TPU v7x, 512 devices: a whole 4x4x16 slice. The times are simulated.
512 devices in a mesh: pos: 16 (over z_lo, x), slab: 32 (over z_hi, y, core).
Axes of the slice: x: 4, y: 4, z: 16 (z_hi: 4, z_lo: 4; z = z_hi * 4 + z_lo), core: 2. Of those that a mesh axis runs over, the one named last changes fastest.
Arguments:
- labels: int32 [64, 256, 256], P('slab'), may hold values from 0 to 3
- magnet_mask: int32 [64, 256, 256], P('slab'), may hold values 0 or 1
- reluctivity: float32 [4], replicated, may hold values from 0.3 to 3
- rotor_shift: int32 [16], P('pos'), may hold values from 0 to 255
- potential: float32 [16, 64, 256, 256], P('pos', 'slab'), may hold values from -6 to 6
- adjoint_load: float32 [16, 64, 256, 256], P('pos', 'slab'), may hold values from -40 to 40
Outputs:
- shape_gradient: float32 [64, 256, 256], P('slab')
- adjoint: float32 [16, 64, 256, 256], P('pos', 'slab')
All inputs are finite; a program needn't handle non-finite values. No bound on the sum of `magnet_mask` on one device may be relied on, other than what follows from the above.
Results may differ from a plain program's by a relative error of at most 0.0003.
Values sent between devices are 32-bit elements; how exact they have to be, the bound alone decides.
A program may use at most 64 MiB of HBM per device.

v0:
```python
import jax
import jax.numpy as jnp
from jax import lax
from jax.sharding import PartitionSpec as P

ITERS = 2
diagonal_shift = 0.5


def padded(shard, sides, width):
    for axis, dim in sides:
        size, length = (lax.axis_size(axis), shard.shape[dim])
        up = [(i, (i + 1) % size) for i in range(size - 1)]
        down = [(j, i) for i, j in up]
        last = lax.slice_in_dim(shard, length - width, length, axis=dim)
        first = lax.slice_in_dim(shard, 0, width, axis=dim)
        before = lax.ppermute(last, axis, up)
        after = lax.ppermute(first, axis, down)
        shard = jnp.concatenate([before, shard, after], axis=dim)
    return shard


def material_field(labels, reluctivity, offset):
    rotated = jnp.roll(labels, offset, axis=2)
    radial = lax.broadcasted_iota(jnp.int32, labels.shape, 1)
    material = jnp.where(radial < labels.shape[1] // 2, rotated, labels)
    result = jnp.zeros(labels.shape, jnp.float32)
    for index in range(4):
        result = result + (material == index).astype(jnp.float32) * reluctivity[index]
    return result


def apply_operator(field, padded_field, relief, padded_relief):
    result = diagonal_shift * field
    result = result + 0.5 * (relief + padded_relief[2:]) * (field - padded_field[2:])
    result = result + 0.5 * (relief + padded_relief[:-2]) * (field - padded_field[:-2])
    radial_field = jnp.pad(field, ((0, 0), (1, 1), (0, 0)))
    radial_relief = jnp.pad(relief, ((0, 0), (1, 1), (0, 0)))
    result = result + 0.5 * (relief + radial_relief[:, 2:]) * (field - radial_field[:, 2:])
    result = result + 0.5 * (relief + radial_relief[:, :-2]) * (field - radial_field[:, :-2])
    for offset in (1, -1):
        result = result + 0.5 * (relief + jnp.roll(relief, offset, 2)) * (
            field - jnp.roll(field, offset, 2)
        )
    return result


def gradient_term(stacked, padded_stack, relief, magnet_mask):
    axial = 0.5 * (padded_stack[:, 2:] - padded_stack[:, :-2])
    radial_pad = jnp.pad(stacked, ((0, 0), (0, 0), (1, 1), (0, 0)))
    radial = 0.5 * (radial_pad[:, :, 2:] - radial_pad[:, :, :-2])
    angular = 0.5 * (jnp.roll(stacked, -1, 3) - jnp.roll(stacked, 1, 3))
    inner = axial[0] * axial[1] + radial[0] * radial[1] + angular[0] * angular[1]
    square = axial[0] * axial[0] + radial[0] * radial[0] + angular[0] * angular[0]
    return magnet_mask.astype(jnp.float32) * relief * (inner + 0.5 * square)


def squares(residual):
    return lax.psum(jnp.sum(residual * residual), "slab")


def local(labels, magnet_mask, reluctivity, rotor_shift, potential, adjoint_load):
    relief = material_field(labels, reluctivity, rotor_shift[0])
    padded_relief = padded(relief, (("slab", 0),), 1)
    solution = jnp.zeros(relief.shape, jnp.float32)
    residual = adjoint_load[0]
    direction = residual
    norm_now = squares(residual)
    for iteration in range(ITERS):
        padded_field = padded(direction, (("slab", 0),), 1)
        image = apply_operator(direction, padded_field, relief, padded_relief)
        alpha = norm_now / lax.psum(jnp.sum(direction * image), "slab")
        solution = solution + alpha * direction
        residual = residual - alpha * image
        norm_next = squares(residual)
        direction = residual + norm_next / norm_now * direction
        norm_now = norm_next
    stacked = jnp.stack([potential[0], solution])
    padded_stack = padded(stacked, (("slab", 1),), 1)
    contribution = gradient_term(stacked, padded_stack, relief, magnet_mask)
    summed = lax.psum(contribution, "pos")
    return (summed / lax.axis_size("pos"), solution[None])


def solution(mesh):
    return jax.shard_map(
        local,
        mesh=mesh,
        in_specs=(
            P("slab", None, None),
            P("slab", None, None),
            P(),
            P("pos"),
            P("pos", "slab", None, None),
            P("pos", "slab", None, None),
        ),
        out_specs=(P("slab", None, None), P("pos", "slab", None, None)),
        check_vma=False,
    )
```

profile of v0, /device:TPU:8, one launch (start us, length us, event | category | flops | bytes accessed | tf_op | source)
XLA Modules:
  0.0 558.1 jit_solution(6151440687633539958)
XLA Ops:
  7.2 0.0 copy-start.8
  7.2 0.0 copy-start.3
  7.2 0.0 all-reduce.7.cloned.1.call-start
  7.2 1.1 slice_bitcast_fusion.1
  8.3 1.9 collective-permute-start.3
  11.0 0.0 copy-done.8
  11.0 0.7 fusion.57
  11.6 0.0 copy-done.3
  11.7 0.0 copy-start
  11.7 3.0 select_add_fusion
  14.7 3.6 collective-permute-start.2
  18.3 2.0 collective-permute-start.1
  20.3 5.6 %collective-permute-start = (f32[1,256,256]{2,1,0:T(8,128)S(1)}, f32[1,256,256]{2,1,0:T(8,128)S(1)}, u32[]{:S(2)}, u32[]{:S(2)}) collective-permute-start(f32[1,256,256]{2,1,0:T(8,128)S(1)} %get-tuple-element.21), channel_id=1, source_target_pairs={{1,0},{2,1},{3,2},{4,3},{5,4},{6,5},{7,6},{8,7},{9,8},{10,9},{11,1... | collective-permute-start | bytes 786440 | tf_op jit(solution)/shard_map/ppermute | solution.py:18
  25.9 0.0 copy-done
  25.9 0.3 fusion.54
  26.2 0.2 fusion.53
  26.4 0.0 collective-permute-done.3
  26.4 0.0 collective-permute-done.2
  26.4 0.0 collective-permute-done.1
  26.5 3.3 collective-permute-done
  29.7 0.0 copy-start.5
  29.7 2.6 multiply_reduce_fusion.1
  32.3 0.0 copy-done.5
  32.3 91.9 %all-reduce.4 = (f32[]{:T(128)}, f32[]{:T(128)}) all-reduce(f32[]{:T(128)} %get-tuple-element.3, f32[]{:T(128)} %get-tuple-element.2), channel_id=1, replica_groups=mesh['pos'=16,'slab'=32] {'slab'}, use_global_device_ids=true, to_apply=%region_1.2 | all-reduce | flops 2 | bytes 16 | tf_op jit(solution)/shard_map/psum | solution.py:59
  125.6 0.7 multiply_reduce_fusion
  126.3 90.4 %psum.37 = f32[]{:T(128)} all-reduce(f32[]{:T(128)} %multiply_reduce_fusion), channel_id=1, replica_groups=mesh['pos'=16,'slab'=32] {'slab'}, use_global_device_ids=true, to_apply=%region_5.6 | all-reduce | flops 1 | bytes 8 | tf_op jit(solution)/shard_map/psum | solution.py:59
  218.0 0.1 multiply_add_fusion
  218.1 0.1 fusion.50
  218.3 2.5 collective-permute-start.5
  220.8 0.0 copy-start.6
  220.8 3.2 collective-permute-start.4
  224.0 0.2 fusion.51
  224.2 1.8 collective-permute-done.5
  226.0 5.7 %collective-permute-done.4 = f32[1,256,256]{2,1,0:T(8,128)S(1)} collective-permute-done((f32[1,256,256]{2,1,0:T(8,128)S(1)}, f32[1,256,256]{2,1,0:T(8,128)S(1)}, u32[]{:S(2)}, u32[]{:S(2)}) %collective-permute-start.4) | collective-permute-done | bytes 262176 | tf_op jit(solution)/shard_map/ppermute | solution.py:18
  231.7 0.0 copy-done.6
  231.7 1.5 fusion.47
  233.2 0.0 copy-start.2
  233.2 89.6 %psum.38 = f32[]{:T(128)} all-reduce(f32[]{:T(128)} %fusion.47), channel_id=1, replica_groups=mesh['pos'=16,'slab'=32] {'slab'}, use_global_device_ids=true, to_apply=%region_7.8 | all-reduce | flops 1 | bytes 8 | tf_op jit(solution)/shard_map/psum | solution.py:72
  324.1 0.1 add_bitcast_fusion
  324.2 0.0 copy-done.2
  324.2 0.0 copy-start.1
  324.2 0.1 fusion.7
  324.3 8.0 %collective-permute-start.7 = (f32[2,1,256,256]{3,2,1,0:T(8,128)S(1)}, f32[2,1,256,256]{3,2,1,0:T(8,128)S(1)}, u32[]{:S(2)}, u32[]{:S(2)}) collective-permute-start(f32[2,1,256,256]{3,2,1,0:T(8,128)S(1)} %get-tuple-element.10), channel_id=1, source_target_pairs={{0,1},{1,2},{2,3},{3,4},{4,5},{5,6},{6,7},{7,8},{8,9},{9,10},{10,1... | collective-permute-start | bytes 1572872 | tf_op jit(solution)/shard_map/ppermute | solution.py:17
  332.4 1.9 collective-permute-start.6
  334.3 0.2 fusion.10
  334.5 0.3 fusion.1
  334.8 0.5 fusion.4
  335.3 0.0 collective-permute-done.7
  335.3 5.6 %collective-permute-done.6 = f32[2,1,256,256]{3,2,1,0:T(8,128)S(1)} collective-permute-done((f32[2,1,256,256]{3,2,1,0:T(8,128)S(1)}, f32[2,1,256,256]{3,2,1,0:T(8,128)S(1)}, u32[]{:S(2)}, u32[]{:S(2)}) %collective-permute-start.6) | collective-permute-done | bytes 524320 | tf_op jit(solution)/shard_map/ppermute | solution.py:18
  341.0 0.0 copy-done.1
  341.0 0.2 fusion.3
  341.2 0.0 copy-start.4
  341.2 0.0 copy-start.7
  341.2 0.2 subtract_multiply_fusion
  341.4 0.8 copy-done.4
  342.2 0.2 copy-done.7
  342.4 4.0 fusion.14
  346.4 0.0 all-reduce.7.cloned.1.call-update
  346.4 203.0 %all-reduce.7.cloned.1.call-done = f32[2,256,256]{2,1,0:T(8,128)} async-done(((f32[2,256,256]{2,1,0:T(8,128)}), f32[2,256,256]{2,1,0:T(8,128)}) %all-reduce.7.cloned.1.call-update) | async-done | bytes 524304 | tf_op jit(solution)/shard_map/psum | solution.py:81
  549.4 1.9 broadcast_multiply_fusion
  (3 shorter events, 0.1 us)
Async XLA Ops:
  7.2 3.8 copy-start.8
  7.2 4.5 copy-start.3
  7.2 542.2 %all-reduce.7.cloned.1.call-start = ((), (), s32[]{:S(2)}) async-start(), calls=%async_computation | async-start | bytes 1048576 | tf_op jit(solution)/shard_map/psum | solution.py:81
  8.3 18.1 %collective-permute-start.3 = (f32[1,256,256]{2,1,0:T(8,128)S(1)}, f32[1,256,256]{2,1,0:T(8,128)}, u32[]{:S(2)}, u32[]{:S(2)}) collective-permute-start(f32[1,256,256]{2,1,0:T(8,128)S(1)} %get-tuple-element.24), channel_id=1, source_target_pairs={{0,1},{1,2},{2,3},{3,4},{4,5},{5,6},{6,7},{7,8},{8,9},{9,10},{10,1... | collective-permute-start | bytes 786440 | tf_op jit(solution)/shard_map/ppermute | solution.py:17
  11.7 14.2 %copy-start = (f32[1,2,256,256]{3,2,1,0:T(8,128)S(1)}, f32[1,2,256,256]{3,2,1,0:T(8,128)}, u32[]{:S(2)}) copy-start(f32[1,2,256,256]{3,2,1,0:T(8,128)} %param.11) | copy-start | bytes 1572868
  14.7 11.7 %collective-permute-start.2 = (f32[1,256,256]{2,1,0:T(8,128)S(1)}, f32[1,256,256]{2,1,0:T(8,128)S(1)}, u32[]{:S(2)}, u32[]{:S(2)}) collective-permute-start(f32[1,256,256]{2,1,0:T(8,128)S(1)} %get-tuple-element.22), channel_id=1, source_target_pairs={{0,1},{1,2},{2,3},{3,4},{4,5},{5,6},{6,7},{7,8},{8,9},{9,10},{10,1... | collective-permute-start | bytes 786440 | tf_op jit(solution)/shard_map/ppermute | solution.py:17
  18.3 8.1 %collective-permute-start.1 = (f32[1,256,256]{2,1,0:T(8,128)S(1)}, f32[1,256,256]{2,1,0:T(8,128)S(1)}, u32[]{:S(2)}, u32[]{:S(2)}) collective-permute-start(f32[1,256,256]{2,1,0:T(8,128)S(1)} %get-tuple-element.23), channel_id=1, source_target_pairs={{1,0},{2,1},{3,2},{4,3},{5,4},{6,5},{7,6},{8,7},{9,8},{10,9},{11,1... | collective-permute-start | bytes 786440 | tf_op jit(solution)/shard_map/ppermute | solution.py:18
  20.3 9.5 %collective-permute-start = (f32[1,256,256]{2,1,0:T(8,128)S(1)}, f32[1,256,256]{2,1,0:T(8,128)S(1)}, u32[]{:S(2)}, u32[]{:S(2)}) collective-permute-start(f32[1,256,256]{2,1,0:T(8,128)S(1)} %get-tuple-element.21), channel_id=1, source_target_pairs={{1,0},{2,1},{3,2},{4,3},{5,4},{6,5},{7,6},{8,7},{9,8},{10,9},{11,1... | collective-permute-start | bytes 786440 | tf_op jit(solution)/shard_map/ppermute | solution.py:18
  29.7 2.6 copy-start.5
  218.3 7.7 %collective-permute-start.5 = (f32[1,256,256]{2,1,0:T(8,128)S(1)}, f32[1,256,256]{2,1,0:T(8,128)S(1)}, u32[]{:S(2)}, u32[]{:S(2)}) collective-permute-start(f32[1,256,256]{2,1,0:T(8,128)S(1)} %get-tuple-element.16), channel_id=1, source_target_pairs={{0,1},{1,2},{2,3},{3,4},{4,5},{5,6},{6,7},{7,8},{8,9},{9,10},{10,1... | collective-permute-start | bytes 786440 | tf_op jit(solution)/shard_map/ppermute | solution.py:17
  220.8 10.9 %copy-start.6 = (f32[1,256,256]{2,1,0:T(8,128)S(1)}, f32[1,256,256]{2,1,0:T(8,128)}, u32[]{:S(2)}) copy-start(f32[1,256,256]{2,1,0:T(8,128)} %copy-done.5) | copy-start | bytes 786436
  220.8 10.8 %collective-permute-start.4 = (f32[1,256,256]{2,1,0:T(8,128)S(1)}, f32[1,256,256]{2,1,0:T(8,128)S(1)}, u32[]{:S(2)}, u32[]{:S(2)}) collective-permute-start(f32[1,256,256]{2,1,0:T(8,128)S(1)} %get-tuple-element.15), channel_id=1, source_target_pairs={{1,0},{2,1},{3,2},{4,3},{5,4},{6,5},{7,6},{8,7},{9,8},{10,9},{11,1... | collective-permute-start | bytes 786440 | tf_op jit(solution)/shard_map/ppermute | solution.py:18
  233.2 91.1 %copy-start.2 = (f32[1,2,256,256]{3,2,1,0:T(8,128)S(1)}, f32[1,2,256,256]{3,2,1,0:T(8,128)}, u32[]{:S(2)}) copy-start(f32[1,2,256,256]{3,2,1,0:T(8,128)} %param.10) | copy-start | bytes 1572868
  324.2 16.7 %copy-start.1 = (f32[1,2,256,256]{3,2,1,0:T(8,128)}, f32[1,2,256,256]{3,2,1,0:T(8,128)S(1)}, u32[]{:S(2)}) copy-start(f32[1,2,256,256]{3,2,1,0:T(8,128)S(1)} %add_bitcast_fusion) | copy-start | bytes 1572868
  324.3 11.0 %collective-permute-start.7 = (f32[2,1,256,256]{3,2,1,0:T(8,128)S(1)}, f32[2,1,256,256]{3,2,1,0:T(8,128)S(1)}, u32[]{:S(2)}, u32[]{:S(2)}) collective-permute-start(f32[2,1,256,256]{3,2,1,0:T(8,128)S(1)} %get-tuple-element.10), channel_id=1, source_target_pairs={{0,1},{1,2},{2,3},{3,4},{4,5},{5,6},{6,7},{7,8},{8,9},{9,10},{10,1... | collective-permute-start | bytes 1572872 | tf_op jit(solution)/shard_map/ppermute | solution.py:17
  332.4 8.6 %collective-permute-start.6 = (f32[2,1,256,256]{3,2,1,0:T(8,128)S(1)}, f32[2,1,256,256]{3,2,1,0:T(8,128)S(1)}, u32[]{:S(2)}, u32[]{:S(2)}) collective-permute-start(f32[2,1,256,256]{3,2,1,0:T(8,128)S(1)} %get-tuple-element.9), channel_id=1, source_target_pairs={{1,0},{2,1},{3,2},{4,3},{5,4},{6,5},{7,6},{8,7},{9,8},{10,9},{11,1... | collective-permute-start | bytes 1572872 | tf_op jit(solution)/shard_map/ppermute | solution.py:18
  341.2 1.0 copy-start.4
  341.2 1.2 copy-start.7
Sparse Core Ops, SparseCore 0:
  346.5 202.8 all-reduce.6
where the time goes:
time: 559 us; the launch traced here: 558 us
  blocking collectives  272 us (49%)
  waiting for transfers between devices  219 us (39%)
  starting transfers between devices  28.7 us (5%)
  between operations  18.9 us (3%)
  other arithmetic  15.4 us (3%)
    psum x1, waiting for transfers between devices, local(): summed = lax.psum(contribution, 'pos')  203 us
    psum x2, blocking collectives, squares(): return lax.psum(jnp.sum(residual * residual), 'slab')  182 us
    psum x1, blocking collectives, local(): alpha = norm_now / lax.psum(jnp.sum(direction * image), 'slab')  89.6 us
    ppermute x4, starting transfers between devices, padded(): before = lax.ppermute(last, axis, up)  16.1 us
    ppermute x4, waiting for transfers between devices, padded(): after = lax.ppermute(first, axis, down)  14.6 us
    ppermute x4, starting transfers between devices, padded(): after = lax.ppermute(first, axis, down)  12.7 us
  transfers between devices with their start and end apart: 9, of which 5 were waited for; matrix products, arithmetic and copies ran while one was open for 1% of the time, Pallas kernels for 0%

commit v1 on v0

--- a/solution.py
+++ b/solution.py
@@ -78,7 +78,7 @@
     stacked = jnp.stack([potential[0], solution])
     padded_stack = padded(stacked, (("slab", 1),), 1)
     contribution = gradient_term(stacked, padded_stack, relief, magnet_mask)
-    summed = lax.psum(contribution, "pos")
+    summed = jnp.sum(lax.all_gather(contribution, "pos"), axis=0)
     return (summed / lax.axis_size("pos"), solution[None])
 
 

time: 559 us -> 502 us (0.90)
  the two profiles are of different devices: /device:TPU:8 before, /device:TPU:1 now
where the time goes in v1:
time: 502 us; the launch traced here: 501 us
  blocking collectives  263 us (52%)
  waiting for transfers between devices  159 us (32%)
  starting transfers between devices  34 us (7%)
  other arithmetic  20.1 us (4%)
  between operations  18.9 us (4%)
  local copies, waits for them, and re-layouts  6.04 us (1%)
    psum x2, blocking collectives, squares(): return lax.psum(jnp.sum(residual * residual), 'slab')  175 us
    all_gather x1, waiting for transfers between devices, local(): summed = jnp.sum(lax.all_gather(contribution, 'pos'), axis=0)  151 us
    psum x1, blocking collectives, local(): alpha = norm_now / lax.psum(jnp.sum(direction * image), 'slab')  87.6 us
    ppermute x4, starting transfers between devices, padded(): after = lax.ppermute(first, axis, down)  25.1 us
  transfers between devices with their start and end apart: 9, of which 5 were waited for; matrix products, arithmetic and copies ran while one was open for 1% of the time, Pallas kernels for 0%

profile of v1, /device:TPU:1, one launch (start us, length us, event | category | flops | bytes accessed | tf_op | source)
XLA Modules:
  0.0 501.1 jit_solution(7463813606836417823)
XLA Ops:
  7.2 0.0 copy-start
  7.2 0.0 all-gather.3.cloned.1.call-start
  8.0 1.5 fusion.57
  9.4 4.5 select_add_fusion
  14.0 8.8 %collective-permute-start = (f32[1,256,256]{2,1,0:T(8,128)S(1)}, f32[1,256,256]{2,1,0:T(8,128)S(1)}, u32[]{:S(2)}, u32[]{:S(2)}) collective-permute-start(f32[1,256,256]{2,1,0:T(8,128)S(1)} %get-tuple-element.21), channel_id=1, source_target_pairs={{1,0},{2,1},{3,2},{4,3},{5,4},{6,5},{7,6},{8,7},{9,8},{10,9},{11,1... | collective-permute-start | bytes 786440 | tf_op jit(solution)/shard_map/ppermute | solution.py:18
  22.8 1.9 collective-permute-start.2
  24.7 1.1 slice_bitcast_fusion.1
  25.7 2.4 collective-permute-start.1
  28.2 3.1 collective-permute-start.3
  31.3 1.6 fusion.54
  32.9 1.2 fusion.53
  34.1 0.0 copy-start.3
  34.2 0.0 collective-permute-done
  34.2 0.0 copy-start.5
  34.2 0.0 collective-permute-done.2
  34.2 0.0 copy-start.6
  34.2 0.0 collective-permute-done.1
  34.2 0.4 collective-permute-done.3
  34.6 0.2 copy-done.3
  34.9 0.0 copy-done
  34.9 1.6 multiply_reduce_fusion.1
  36.5 0.0 copy-done.5
  36.5 0.0 copy-start.2
  36.5 0.0 copy-done.6
  36.5 89.0 %all-reduce.4 = (f32[]{:T(128)}, f32[]{:T(128)}) all-reduce(f32[]{:T(128)} %get-tuple-element.3, f32[]{:T(128)} %get-tuple-element.2), channel_id=1, replica_groups=mesh['pos'=16,'slab'=32] {'slab'}, use_global_device_ids=true, to_apply=%region_1.2 | all-reduce | flops 2 | bytes 16 | tf_op jit(solution)/shard_map/psum | solution.py:59
  126.7 0.8 multiply_reduce_fusion
  127.5 86.4 %psum.30 = f32[]{:T(128)} all-reduce(f32[]{:T(128)} %multiply_reduce_fusion), channel_id=1, replica_groups=mesh['pos'=16,'slab'=32] {'slab'}, use_global_device_ids=true, to_apply=%region_5.6 | all-reduce | flops 1 | bytes 8 | tf_op jit(solution)/shard_map/psum | solution.py:59
  215.2 0.1 multiply_add_fusion
  215.3 0.1 fusion.50
  215.5 8.0 %collective-permute-start.4 = (f32[1,256,256]{2,1,0:T(8,128)S(1)}, f32[1,256,256]{2,1,0:T(8,128)S(1)}, u32[]{:S(2)}, u32[]{:S(2)}) collective-permute-start(f32[1,256,256]{2,1,0:T(8,128)S(1)} %get-tuple-element.15), channel_id=1, source_target_pairs={{1,0},{2,1},{3,2},{4,3},{5,4},{6,5},{7,6},{8,7},{9,8},{10,9},{11,1... | collective-permute-start | bytes 786440 | tf_op jit(solution)/shard_map/ppermute | solution.py:18
  223.5 1.9 collective-permute-start.5
  225.4 0.2 fusion.51
  225.6 0.0 collective-permute-done.4
  225.6 3.1 collective-permute-done.5
  228.7 2.6 fusion.47
  231.3 87.6 %psum.31 = f32[]{:T(128)} all-reduce(f32[]{:T(128)} %fusion.47), channel_id=1, replica_groups=mesh['pos'=16,'slab'=32] {'slab'}, use_global_device_ids=true, to_apply=%region_7.8 | all-reduce | flops 1 | bytes 8 | tf_op jit(solution)/shard_map/psum | solution.py:72
  320.2 0.1 add_bitcast_fusion
  320.4 0.0 copy-done.2
  320.4 0.0 copy-start.1
  320.4 0.1 fusion.7
  320.5 0.0 copy-start.4
  320.5 0.0 copy-start.7
  320.5 5.9 %collective-permute-start.6 = (f32[2,1,256,256]{3,2,1,0:T(8,128)S(1)}, f32[2,1,256,256]{3,2,1,0:T(8,128)S(1)}, u32[]{:S(2)}, u32[]{:S(2)}) collective-permute-start(f32[2,1,256,256]{3,2,1,0:T(8,128)S(1)} %get-tuple-element.9), channel_id=1, source_target_pairs={{1,0},{2,1},{3,2},{4,3},{5,4},{6,5},{7,6},{8,7},{9,8},{10,9},{11,1... | collective-permute-start | bytes 1572872 | tf_op jit(solution)/shard_map/ppermute | solution.py:18
  326.4 1.9 collective-permute-start.7
  328.3 0.2 fusion.10
  328.5 0.3 fusion.1
  328.9 0.5 fusion.4
  329.3 1.8 collective-permute-done.6
  331.1 3.3 collective-permute-done.7
  334.4 0.2 fusion.3
  334.6 0.2 subtract_multiply_fusion
  334.8 0.0 copy-done.1
  334.9 0.0 copy-done.4
  334.9 0.0 copy-done.7
  334.9 4.0 fusion.14
  338.9 0.0 all-gather.3.cloned.1.call-update
  338.9 150.5 %all-gather.3.cloned.1.call-done = f32[32,256,256]{2,1,0:T(8,128)} async-done(((f32[2,256,256]{2,1,0:T(8,128)}), f32[32,256,256]{2,1,0:T(8,128)}) %all-gather.3.cloned.1.call-update) | async-done | bytes 8388624 | tf_op jit(solution)/shard_map/all_gather | solution.py:81
  489.5 4.0 reduce_sum.49
  493.4 0.8 broadcast_multiply_fusion
  (3 shorter events, 0.1 us)
Async XLA Ops:
  7.2 27.7 %copy-start = (f32[1,2,256,256]{3,2,1,0:T(8,128)S(1)}, f32[1,2,256,256]{3,2,1,0:T(8,128)}, u32[]{:S(2)}) copy-start(f32[1,2,256,256]{3,2,1,0:T(8,128)} %param.11) | copy-start | bytes 1572868
  7.2 482.3 %all-gather.3.cloned.1.call-start = ((), (), s32[]{:S(2)}) async-start(), calls=%async_computation | async-start | bytes 8912896 | tf_op jit(solution)/shard_map/all_gather | solution.py:81
  14.0 20.2 %collective-permute-start = (f32[1,256,256]{2,1,0:T(8,128)S(1)}, f32[1,256,256]{2,1,0:T(8,128)S(1)}, u32[]{:S(2)}, u32[]{:S(2)}) collective-permute-start(f32[1,256,256]{2,1,0:T(8,128)S(1)} %get-tuple-element.21), channel_id=1, source_target_pairs={{1,0},{2,1},{3,2},{4,3},{5,4},{6,5},{7,6},{8,7},{9,8},{10,9},{11,1... | collective-permute-start | bytes 786440 | tf_op jit(solution)/shard_map/ppermute | solution.py:18
  22.8 11.4 %collective-permute-start.2 = (f32[1,256,256]{2,1,0:T(8,128)S(1)}, f32[1,256,256]{2,1,0:T(8,128)S(1)}, u32[]{:S(2)}, u32[]{:S(2)}) collective-permute-start(f32[1,256,256]{2,1,0:T(8,128)S(1)} %get-tuple-element.22), channel_id=1, source_target_pairs={{0,1},{1,2},{2,3},{3,4},{4,5},{5,6},{6,7},{7,8},{8,9},{9,10},{10,1... | collective-permute-start | bytes 786440 | tf_op jit(solution)/shard_map/ppermute | solution.py:17
  25.7 8.5 %collective-permute-start.1 = (f32[1,256,256]{2,1,0:T(8,128)S(1)}, f32[1,256,256]{2,1,0:T(8,128)S(1)}, u32[]{:S(2)}, u32[]{:S(2)}) collective-permute-start(f32[1,256,256]{2,1,0:T(8,128)S(1)} %get-tuple-element.23), channel_id=1, source_target_pairs={{1,0},{2,1},{3,2},{4,3},{5,4},{6,5},{7,6},{8,7},{9,8},{10,9},{11,1... | collective-permute-start | bytes 786440 | tf_op jit(solution)/shard_map/ppermute | solution.py:18
  28.2 6.4 %collective-permute-start.3 = (f32[1,256,256]{2,1,0:T(8,128)S(1)}, f32[1,256,256]{2,1,0:T(8,128)S(1)}, u32[]{:S(2)}, u32[]{:S(2)}) collective-permute-start(f32[1,256,256]{2,1,0:T(8,128)S(1)} %get-tuple-element.24), channel_id=1, source_target_pairs={{0,1},{1,2},{2,3},{3,4},{4,5},{5,6},{6,7},{7,8},{8,9},{9,10},{10,1... | collective-permute-start | bytes 786440 | tf_op jit(solution)/shard_map/ppermute | solution.py:17
  34.1 0.7 copy-start.3
  34.2 2.3 copy-start.5
  34.2 2.3 copy-start.6
  36.5 283.9 %copy-start.2 = (f32[1,2,256,256]{3,2,1,0:T(8,128)S(1)}, f32[1,2,256,256]{3,2,1,0:T(8,128)}, u32[]{:S(2)}) copy-start(f32[1,2,256,256]{3,2,1,0:T(8,128)} %param.10) | copy-start | bytes 1572868
  215.5 10.2 %collective-permute-start.4 = (f32[1,256,256]{2,1,0:T(8,128)S(1)}, f32[1,256,256]{2,1,0:T(8,128)S(1)}, u32[]{:S(2)}, u32[]{:S(2)}) collective-permute-start(f32[1,256,256]{2,1,0:T(8,128)S(1)} %get-tuple-element.15), channel_id=1, source_target_pairs={{1,0},{2,1},{3,2},{4,3},{5,4},{6,5},{7,6},{8,7},{9,8},{10,9},{11,1... | collective-permute-start | bytes 786440 | tf_op jit(solution)/shard_map/ppermute | solution.py:18
  223.5 5.2 %collective-permute-start.5 = (f32[1,256,256]{2,1,0:T(8,128)S(1)}, f32[1,256,256]{2,1,0:T(8,128)S(1)}, u32[]{:S(2)}, u32[]{:S(2)}) collective-permute-start(f32[1,256,256]{2,1,0:T(8,128)S(1)} %get-tuple-element.16), channel_id=1, source_target_pairs={{0,1},{1,2},{2,3},{3,4},{4,5},{5,6},{6,7},{7,8},{8,9},{9,10},{10,1... | collective-permute-start | bytes 786440 | tf_op jit(solution)/shard_map/ppermute | solution.py:17
  320.4 14.5 %copy-start.1 = (f32[1,2,256,256]{3,2,1,0:T(8,128)}, f32[1,2,256,256]{3,2,1,0:T(8,128)S(1)}, u32[]{:S(2)}) copy-start(f32[1,2,256,256]{3,2,1,0:T(8,128)S(1)} %add_bitcast_fusion) | copy-start | bytes 1572868
  320.5 14.4 %copy-start.4 = (s32[2,256,256]{2,1,0:T(8,128)S(1)}, s32[2,256,256]{2,1,0:T(8,128)}, u32[]{:S(2)}) copy-start(s32[2,256,256]{2,1,0:T(8,128)} %param.6) | copy-start | bytes 1572868
  320.5 14.4 %copy-start.7 = (s32[2,256,256]{2,1,0:T(8,128)S(1)}, s32[2,256,256]{2,1,0:T(8,128)}, u32[]{:S(2)}) copy-start(s32[2,256,256]{2,1,0:T(8,128)} %param.7) | copy-start | bytes 1572868
  320.5 10.6 %collective-permute-start.6 = (f32[2,1,256,256]{3,2,1,0:T(8,128)S(1)}, f32[2,1,256,256]{3,2,1,0:T(8,128)S(1)}, u32[]{:S(2)}, u32[]{:S(2)}) collective-permute-start(f32[2,1,256,256]{3,2,1,0:T(8,128)S(1)} %get-tuple-element.9), channel_id=1, source_target_pairs={{1,0},{2,1},{3,2},{4,3},{5,4},{6,5},{7,6},{8,7},{9,8},{10,9},{11,1... | collective-permute-start | bytes 1572872 | tf_op jit(solution)/shard_map/ppermute | solution.py:18
  326.4 8.0 %collective-permute-start.7 = (f32[2,1,256,256]{3,2,1,0:T(8,128)S(1)}, f32[2,1,256,256]{3,2,1,0:T(8,128)S(1)}, u32[]{:S(2)}, u32[]{:S(2)}) collective-permute-start(f32[2,1,256,256]{3,2,1,0:T(8,128)S(1)} %get-tuple-element.10), channel_id=1, source_target_pairs={{0,1},{1,2},{2,3},{3,4},{4,5},{5,6},{6,7},{7,8},{8,9},{9,10},{10,1... | collective-permute-start | bytes 1572872 | tf_op jit(solution)/shard_map/ppermute | solution.py:17
Sparse Core Ops, SparseCore 0:
  339.1 150.3 all-gather.2
